TPU v7x, 32 devices: a whole 2x2x4 slice. The times are simulated.
32 devices in a mesh: dp: 8 (over z, x), mp: 4 (over y, core).
Axes of the slice: x: 2, y: 2, z: 4, core: 2. Of those that a mesh axis runs over, the one named last changes fastest.
Arguments:
- tokens: float32 [10240, 1024], P(('dp', 'mp')), may hold values from -6 to 6
- cotangent: float32 [10240, 1024], P(('dp', 'mp')), may hold values from -6 to 6
- segments: int32 [10240], P('dp'), may hold values from 0 to 63, as said below
- attention_weights: float32 [2, 4, 1024, 1024], P(None, None, 'dp', 'mp')
- attention_first: float32 [2, 4, 1024, 1024], P(None, None, 'dp', 'mp')
- attention_second: float32 [2, 4, 1024, 1024], P(None, None, 'dp', 'mp')
- dense_weights: float32 [2, 2, 1024, 4096], P(None, None, 'dp', 'mp')
- dense_first: float32 [2, 2, 1024, 4096], P(None, None, 'dp', 'mp')
- dense_second: float32 [2, 2, 1024, 4096], P(None, None, 'dp', 'mp')
- norm_params: float32 [2, 4, 1024], replicated
- norm_first: float32 [2, 4, 1024], replicated
- norm_second: float32 [2, 4, 1024], replicated
Outputs:
- outcome: float32 [10240, 1024], P(('dp', 'mp'))
- grad_tokens: float32 [10240, 1024], P(('dp', 'mp'))
- attention_new: float32 [2, 4, 1024, 1024], P(None, None, 'dp', 'mp')
- attention_first_new: float32 [2, 4, 1024, 1024], P(None, None, 'dp', 'mp')
- attention_second_new: float32 [2, 4, 1024, 1024], P(None, None, 'dp', 'mp')
- attention_copy: bfloat16 [2, 4, 1024, 1024], P(None, None, 'dp', 'mp')
- dense_new: float32 [2, 2, 1024, 4096], P(None, None, 'dp', 'mp')
- dense_first_new: float32 [2, 2, 1024, 4096], P(None, None, 'dp', 'mp')
- dense_second_new: float32 [2, 2, 1024, 4096], P(None, None, 'dp', 'mp')
- dense_copy: bfloat16 [2, 2, 1024, 4096], P(None, None, 'dp', 'mp')
- norm_new: float32 [2, 4, 1024], replicated
- norm_first_new: float32 [2, 4, 1024], replicated
- norm_second_new: float32 [2, 4, 1024], replicated
- norms: float32 [2, 6, 2], replicated
- second_norm_grad: float32 [2, 2, 1024], replicated
Inputs may be any that keep to these rules, and one draw needn't show every extreme that they name: `segments`: in each aligned block of 1280 tokens crop numbers start at 0 and never fall; a block holds 2·8 crops of 50 tokens and 6·8 crops of 10 tokens in an order drawn from the seed.
All inputs are finite; a program needn't handle non-finite values.
Results may differ from a plain program's by a relative error of at most 0.029.
Values may be sent and summed in bfloat16 or wider, within the bound.
No kernel may reach another device: no remote copies, remote signals or barrier semaphores. Data moves between devices by JAX's collectives and lax.ppermute only.
A program may use at most 320 MiB of HBM per device.

v0:
```python
import jax
import jax.numpy as jnp
from jax import lax
from jax.sharding import PartitionSpec as P

D = 1024
HEADS = 16
HD = 64
FF = 4096
STEP = 10
EPS_NORM = 1e-06
BETA_ONE = 0.9
BETA_TWO = 0.999
ADAM_EPS = 1e-06
WEIGHT_DECAY = 0.01
LEARN_RATE = 0.5
MASKED = -1000000000.0


def layer_norm(stream, gain, shift):
    centre = stream - jnp.mean(stream, axis=-1, keepdims=True)
    spread = jnp.mean(centre * centre, axis=-1, keepdims=True)
    return centre * lax.rsqrt(spread + EPS_NORM) * gain + shift


def gelu_exact(values_in):
    return jax.nn.gelu(values_in, approximate=False)


def adam_part(gradient, weight, first, second, decay):
    first_new = BETA_ONE * first + (1.0 - BETA_ONE) * gradient
    second_new = BETA_TWO * second + (1.0 - BETA_TWO) * gradient * gradient
    step_dir = (
        first_new
        / (1.0 - BETA_ONE**STEP)
        / (jnp.sqrt(second_new / (1.0 - BETA_TWO**STEP)) + ADAM_EPS)
        + decay * weight
    )
    return (first_new, second_new, step_dir)


def masked_scores(query, keys_in, same_crop):
    scores = jnp.einsum(
        "qhe,khe->hqk", query, keys_in, preferred_element_type=jnp.float32
    ) * HD ** (-0.5)
    return jnp.where(same_crop, scores, MASKED)


def attend(query, keys_in, values_in, same_crop):
    scores = masked_scores(query, keys_in, same_crop)
    row_max = jnp.max(scores, axis=-1, keepdims=True)
    powered = jnp.exp(scores - row_max)
    row_sum = jnp.sum(powered, axis=-1, keepdims=True)
    shares = (powered / row_sum).astype(jnp.bfloat16)
    attended = jnp.einsum("hqk,khe->qhe", shares, values_in, preferred_element_type=jnp.float32)
    return (attended, row_max + jnp.log(row_sum))


def attend_back(query, keys_in, values_in, same_crop, log_total, grad_attended):
    shares = jnp.exp(masked_scores(query, keys_in, same_crop) - log_total)
    grad_shares = jnp.einsum(
        "qhe,khe->hqk", grad_attended, values_in, preferred_element_type=jnp.float32
    )
    row_inner = jnp.sum(grad_shares * shares, axis=-1, keepdims=True)
    grad_scores = (shares * (grad_shares - row_inner)).astype(jnp.bfloat16)
    score_scale = HD ** (-0.5)
    grad_query = (
        jnp.einsum("hqk,khe->qhe", grad_scores, keys_in, preferred_element_type=jnp.float32)
        * score_scale
    )
    grad_keys = (
        jnp.einsum("hqk,qhe->khe", grad_scores, query, preferred_element_type=jnp.float32)
        * score_scale
    )
    grad_values = jnp.einsum(
        "hqk,qhe->khe",
        shares.astype(jnp.bfloat16),
        grad_attended,
        preferred_element_type=jnp.float32,
    )
    return jnp.stack([grad_query, grad_keys, grad_values], axis=1)


def shards(
    tokens,
    cotangent,
    segments,
    attention_weights,
    attention_first,
    attention_second,
    dense_weights,
    dense_first,
    dense_second,
    norm_params,
    norm_first,
    norm_second,
):
    layers = attention_weights.shape[0]
    token_count = segments.shape[0]
    heads_here = attention_weights.shape[3] // HD
    same_crop = (segments[:, None] == segments[None, :])[None]
    mixer_low = attention_weights.astype(jnp.bfloat16)
    dense_low = dense_weights.astype(jnp.bfloat16)
    copies = []
    for current in range(layers):
        copies.append(
            (
                lax.all_gather(mixer_low[current], "dp", axis=1, tiled=True),
                lax.all_gather(dense_low[current], "dp", axis=1, tiled=True),
            )
        )
    saved_forward = []
    stream = tokens
    for current in range(layers):
        mixer_full, dense_full = copies[current]
        params = norm_params[current]
        normed = layer_norm(stream, params[0], params[1]).astype(jnp.bfloat16)
        gathered = lax.all_gather(normed, "mp", axis=0, tiled=True)
        projected = jnp.einsum(
            "td,sdh->tsh", gathered, mixer_full[:3], preferred_element_type=jnp.float32
        ).astype(jnp.bfloat16)
        split_heads = projected.reshape(token_count, 3, heads_here, HD)
        attended, log_total = attend(
            split_heads[:, 0], split_heads[:, 1], split_heads[:, 2], same_crop
        )
        attended = attended.reshape(token_count, heads_here * HD).astype(jnp.bfloat16)
        middle = stream + lax.psum_scatter(
            jnp.einsum(
                "th,dh->td", attended, mixer_full[3], preferred_element_type=jnp.float32
            ).astype(jnp.bfloat16),
            "mp",
            scatter_dimension=0,
            tiled=True,
        ).astype(jnp.float32)
        normed_two = layer_norm(middle, params[2], params[3]).astype(jnp.bfloat16)
        dense_wide = dense_full
        gathered_two = lax.all_gather(normed_two, "mp", axis=0, tiled=True)
        hidden = jnp.dot(gathered_two, dense_full[0], preferred_element_type=jnp.float32)
        active = gelu_exact(hidden).astype(jnp.bfloat16)
        after_dense = middle + lax.psum_scatter(
            jnp.einsum(
                "tf,df->td", active, dense_full[1], preferred_element_type=jnp.float32
            ).astype(jnp.bfloat16),
            "mp",
            scatter_dimension=0,
            tiled=True,
        ).astype(jnp.float32)
        saved_forward.append(
            (
                stream,
                gathered,
                projected,
                log_total,
                attended,
                middle,
                gathered_two,
                hidden,
                active,
                dense_wide,
            )
        )
        stream = after_dense
    stream_grad = cotangent
    states = [None] * layers
    squares_list = [None] * layers
    vector_list = [None] * layers
    summed_list = [None] * layers
    for current in reversed(range(layers)):
        (
            stream_in,
            gathered,
            projected,
            log_total,
            attended,
            middle,
            gathered_two,
            hidden,
            active,
            dense_wide,
        ) = saved_forward[current]
        mixer_full, dense_full = copies[current]
        params = norm_params[current]
        back_rows = lax.all_gather(stream_grad.astype(jnp.bfloat16), "mp", axis=0, tiled=True)
        grad_active = jnp.dot(back_rows, dense_full[1], preferred_element_type=jnp.float32)
        grad_down = jnp.einsum("td,tf->df", back_rows, active, preferred_element_type=jnp.float32)
        gelu_value, gelu_pull = jax.vjp(gelu_exact, hidden)
        grad_hidden = gelu_pull(grad_active)[0].astype(jnp.bfloat16)
        grad_up = jnp.einsum(
            "td,tf->df", gathered_two, grad_hidden, preferred_element_type=jnp.float32
        )
        grad_normed_two = lax.psum_scatter(
            jnp.einsum(
                "tf,df->td", grad_hidden, dense_full[0], preferred_element_type=jnp.float32
            ).astype(jnp.bfloat16),
            "mp",
            scatter_dimension=0,
            tiled=True,
        ).astype(jnp.float32)
        norm_value, norm_pull = jax.vjp(layer_norm, middle, params[2], params[3])
        grad_middle, grad_gain_two, grad_shift_two = norm_pull(grad_normed_two)
        stream_grad = stream_grad + grad_middle
        back_rows_two = lax.all_gather(stream_grad.astype(jnp.bfloat16), "mp", axis=0, tiled=True)
        grad_attended = jnp.dot(
            back_rows_two, mixer_full[3], preferred_element_type=jnp.float32
        ).astype(jnp.bfloat16)
        grad_output_map = jnp.einsum(
            "td,th->dh", back_rows_two, attended, preferred_element_type=jnp.float32
        )
        split_heads = projected.reshape(token_count, 3, heads_here, HD)
        grad_split = attend_back(
            split_heads[:, 0],
            split_heads[:, 1],
            split_heads[:, 2],
            same_crop,
            log_total,
            grad_attended.reshape(token_count, heads_here, HD),
        )
        grad_projected = grad_split.reshape(token_count, 3, heads_here * HD).astype(jnp.bfloat16)
        grad_inputs_map = jnp.einsum(
            "td,tsh->sdh", gathered, grad_projected, preferred_element_type=jnp.float32
        )
        grad_normed = lax.psum_scatter(
            jnp.einsum(
                "tsh,sdh->td", grad_projected, mixer_full[:3], preferred_element_type=jnp.float32
            ).astype(jnp.bfloat16),
            "mp",
            scatter_dimension=0,
            tiled=True,
        ).astype(jnp.float32)
        norm_value_one, norm_pull_one = jax.vjp(layer_norm, stream_in, params[0], params[1])
        grad_inner, grad_gain_one, grad_shift_one = norm_pull_one(grad_normed)
        stream_grad = stream_grad + grad_inner
        mixer_grad = jnp.concatenate([grad_inputs_map, grad_output_map[None]], axis=0)
        dense_grad = jnp.stack([grad_up, grad_down], axis=0)
        mixer_grad, dense_grad = (
            lax.psum_scatter(mixer_grad, "dp", scatter_dimension=1, tiled=True),
            lax.psum_scatter(dense_grad, "dp", scatter_dimension=1, tiled=True),
        )
        mixer_first, mixer_second, mixer_step = adam_part(
            mixer_grad,
            attention_weights[current],
            attention_first[current],
            attention_second[current],
            WEIGHT_DECAY,
        )
        dense_first_new, dense_second_new, dense_step = adam_part(
            dense_grad,
            dense_weights[current],
            dense_first[current],
            dense_second[current],
            WEIGHT_DECAY,
        )
        weight_squares = jnp.concatenate(
            [
                jnp.sum(attention_weights[current] * attention_weights[current], axis=(1, 2)),
                jnp.sum(dense_weights[current] * dense_weights[current], axis=(1, 2)),
            ]
        )
        step_squares = jnp.concatenate(
            [
                jnp.sum(mixer_step * mixer_step, axis=(1, 2)),
                jnp.sum(dense_step * dense_step, axis=(1, 2)),
            ]
        )
        squares = jnp.stack([weight_squares, step_squares], axis=-1)
        vector_grad = jnp.stack(
            [grad_gain_one, grad_shift_one, grad_gain_two, grad_shift_two], axis=0
        )
        states[current] = (
            mixer_first,
            mixer_second,
            mixer_step,
            dense_first_new,
            dense_second_new,
            dense_step,
        )
        squares_list[current] = squares
        vector_list[current] = vector_grad
        summed_list[current] = lax.psum((squares, vector_grad), ("dp", "mp"))
    total_squares = jnp.stack([entry[0] for entry in summed_list])
    total_vectors = jnp.stack([entry[1] for entry in summed_list])
    sizes_all = jnp.sqrt(total_squares[:, :, 0])
    moves_all = jnp.sqrt(total_squares[:, :, 1])
    trust_all = sizes_all / moves_all
    mixer_new = jnp.stack(
        [
            attention_weights[current]
            - LEARN_RATE * trust_all[current, :4, None, None] * states[current][2]
            for current in range(layers)
        ]
    )
    dense_new = jnp.stack(
        [
            dense_weights[current]
            - LEARN_RATE * trust_all[current, 4:, None, None] * states[current][5]
            for current in range(layers)
        ]
    )
    mixer_first_all = jnp.stack([states[current][0] for current in range(layers)])
    mixer_second_all = jnp.stack([states[current][1] for current in range(layers)])
    dense_first_all = jnp.stack([states[current][3] for current in range(layers)])
    dense_second_all = jnp.stack([states[current][4] for current in range(layers)])
    params_first, params_second, params_step = adam_part(
        total_vectors, norm_params, norm_first, norm_second, 0.0
    )
    params_size = jnp.sqrt(jnp.sum(norm_params * norm_params, axis=-1))
    params_move = jnp.sqrt(jnp.sum(params_step * params_step, axis=-1))
    params_new = norm_params - LEARN_RATE * (params_size / params_move)[:, :, None] * params_step
    mixer_entries = float(D * HEADS * HD) ** 0.5
    dense_entries = float(D * FF) ** 0.5
    entry_roots = jnp.array([mixer_entries] * 4 + [dense_entries] * 2, jnp.float32)
    norms = jnp.stack([sizes_all / entry_roots[None, :], moves_all / entry_roots[None, :]], axis=-1)
    second_norm_grad = total_vectors[:, 2:4]
    return (
        stream,
        stream_grad,
        mixer_new,
        mixer_first_all,
        mixer_second_all,
        mixer_new.astype(jnp.bfloat16),
        dense_new,
        dense_first_all,
        dense_second_all,
        dense_new.astype(jnp.bfloat16),
        params_new,
        params_first,
        params_second,
        norms,
        second_norm_grad,
    )


def solution(mesh):
    in_specs = (
        P(("dp", "mp"), None),
        P(("dp", "mp"), None),
        P("dp"),
        P(None, None, "dp", "mp"),
        P(None, None, "dp", "mp"),
        P(None, None, "dp", "mp"),
        P(None, None, "dp", "mp"),
        P(None, None, "dp", "mp"),
        P(None, None, "dp", "mp"),
        P(),
        P(),
        P(),
    )
    out_specs = (
        P(("dp", "mp"), None),
        P(("dp", "mp"), None),
        P(None, None, "dp", "mp"),
        P(None, None, "dp", "mp"),
        P(None, None, "dp", "mp"),
        P(None, None, "dp", "mp"),
        P(None, None, "dp", "mp"),
        P(None, None, "dp", "mp"),
        P(None, None, "dp", "mp"),
        P(None, None, "dp", "mp"),
        P(),
        P(),
        P(),
        P(),
        P(),
    )
    return jax.shard_map(shards, mesh=mesh, in_specs=in_specs, out_specs=out_specs, check_vma=False)
```

profile of v0, /device:TPU:0, one launch (start us, length us, event | category | flops | bytes accessed | tf_op | source)
XLA Modules:
  0.0 1625.0 jit_solution(6079072630626825102)
XLA Ops:
  13.5 51.0 %all-gather.33.cloned.1.call-done = bf16[1,4,1024,256]{2,3,1,0:T(8,128)(2,1)} async-done(((bf16[1,4,128,256]{2,3,1,0:T(8,128)(2,1)}), bf16[1,4,1024,256]{2,3,1,0:T(8,128)(2,1)}) %all-gather.33.cloned.1.call-update) | async-done | bytes 2097168 | tf_op jit(solution)/shard_map/all_gather | solution.py:108
  64.4 25.9 %all-gather.17.cloned.1.call-done = bf16[1280,1024]{1,0:T(8,128)(2,1)} async-done(((bf16[320,1024]{1,0:T(8,128)(2,1)}), bf16[1280,1024]{1,0:T(8,128)(2,1)}) %all-gather.17.cloned.1.call-update) | async-done | bytes 2621456 | tf_op jit(solution)/shard_map/all_gather | solution.py:118
  94.8 11.0 fusion.121
  116.5 11.0 fusion.43
  133.2 33.5 %reduce-scatter.13.cloned.1.call-done = bf16[320,1024]{1,0:T(8,128)(2,1)} async-done(((bf16[1280,1024]{1,0:T(8,128)(2,1)}), bf16[320,1024]{1,0:T(8,128)(2,1)}) %reduce-scatter.13.cloned.1.call-update) | async-done | bytes 655376 | tf_op jit(solution)/shard_map/reduce_scatter | solution.py:127
  179.9 63.0 %all-gather.35.cloned.1.call-done = bf16[1,2,1024,1024]{3,2,1,0:T(8,128)(2,1)} async-done(((bf16[1,2,128,1024]{3,2,1,0:T(8,128)(2,1)}), bf16[1,2,1024,1024]{3,2,1,0:T(8,128)(2,1)}) %all-gather.35.cloned.1.call-update) | async-done | bytes 4194320 | tf_op jit(solution)/shard_map/all_gather | solution.py:109
  243.0 25.9 %all-gather.19.cloned.1.call-done = bf16[1280,1024]{1,0:T(8,128)(2,1)} async-done(((bf16[320,1024]{1,0:T(8,128)(2,1)}), bf16[1280,1024]{1,0:T(8,128)(2,1)}) %all-gather.19.cloned.1.call-update) | async-done | bytes 2621456 | tf_op jit(solution)/shard_map/all_gather | solution.py:137
  268.9 17.2 %multiply_convert_fusion.3 = (bf16[1280,1024]{1,0:T(8,128)(2,1)S(1)}, f32[1280,1024]{1,0:T(8,128)}, f32[1280,1024]{1,0:T(8,128)}) fusion(bf16[1280,1024]{1,0:T(8,128)(2,1)} %all-gather.19.cloned.1.call-done, bf16[1,2,1024,1024]{3,2,1,0:T(8,128)(2,1)} %all-gather.35.cloned.1.call-done), kind=kOutput, calls=%fused_computation.47 | convolution fusion | flops 2769551360 | bytes 17825792 | tf_op jit(solution)/shard_map/dot_general | solution.py:138
  292.7 34.0 %reduce-scatter.15.cloned.1.call-done = bf16[320,1024]{1,0:T(8,128)(2,1)} async-done(((bf16[1280,1024]{1,0:T(8,128)(2,1)}), bf16[320,1024]{1,0:T(8,128)(2,1)}) %reduce-scatter.15.cloned.1.call-update) | async-done | bytes 655376 | tf_op jit(solution)/shard_map/reduce_scatter | solution.py:140
  329.6 50.9 %all-gather.37.cloned.1.call-done = bf16[1,4,1024,256]{2,3,1,0:T(8,128)(2,1)} async-done(((bf16[1,4,128,256]{2,3,1,0:T(8,128)(2,1)}), bf16[1,4,1024,256]{2,3,1,0:T(8,128)(2,1)}) %all-gather.37.cloned.1.call-update) | async-done | bytes 2097168 | tf_op jit(solution)/shard_map/all_gather | solution.py:108
  380.4 25.9 %all-gather.21.cloned.1.call-done = bf16[1280,1024]{1,0:T(8,128)(2,1)} async-done(((bf16[320,1024]{1,0:T(8,128)(2,1)}), bf16[1280,1024]{1,0:T(8,128)(2,1)}) %all-gather.21.cloned.1.call-update) | async-done | bytes 2621456 | tf_op jit(solution)/shard_map/all_gather | solution.py:118
  448.3 34.2 %reduce-scatter.17.cloned.1.call-done = bf16[320,1024]{1,0:T(8,128)(2,1)} async-done(((bf16[1280,1024]{1,0:T(8,128)(2,1)}), bf16[320,1024]{1,0:T(8,128)(2,1)}) %reduce-scatter.17.cloned.1.call-update) | async-done | bytes 655376 | tf_op jit(solution)/shard_map/reduce_scatter | solution.py:127
  488.1 70.7 %all-gather.39.cloned.1.call-done = bf16[1,2,1024,1024]{3,2,1,0:T(8,128)(2,1)} async-done(((bf16[1,2,128,1024]{3,2,1,0:T(8,128)(2,1)}), bf16[1,2,1024,1024]{3,2,1,0:T(8,128)(2,1)}) %all-gather.39.cloned.1.call-update) | async-done | bytes 4194320 | tf_op jit(solution)/shard_map/all_gather | solution.py:109
  558.8 26.1 %all-gather.23.cloned.1.call-done = bf16[1280,1024]{1,0:T(8,128)(2,1)} async-done(((bf16[320,1024]{1,0:T(8,128)(2,1)}), bf16[1280,1024]{1,0:T(8,128)(2,1)}) %all-gather.23.cloned.1.call-update) | async-done | bytes 2621456 | tf_op jit(solution)/shard_map/all_gather | solution.py:137
  584.9 17.3 %multiply_convert_fusion.2 = (bf16[1280,1024]{1,0:T(8,128)(2,1)}, f32[1280,1024]{1,0:T(8,128)}, f32[1280,1024]{1,0:T(8,128)}) fusion(bf16[1280,1024]{1,0:T(8,128)(2,1)} %all-gather.23.cloned.1.call-done, bf16[1,2,1024,1024]{3,2,1,0:T(8,128)(2,1)} %all-gather.39.cloned.1.call-done), kind=kOutput, calls=%fused_computation.34 | convolution fusion | flops 2769551360 | bytes 17825792 | tf_op jit(solution)/shard_map/dot_general | solution.py:138
  635.0 27.9 %reduce-scatter.21.cloned.1.call-done = bf16[320,1024]{1,0:T(8,128)(2,1)} async-done(((bf16[1280,1024]{1,0:T(8,128)(2,1)}), bf16[320,1024]{1,0:T(8,128)(2,1)}) %reduce-scatter.21.cloned.1.call-update) | async-done | bytes 655376 | tf_op jit(solution)/shard_map/reduce_scatter | solution.py:191
  665.2 34.9 %reduce-scatter.19.cloned.1.call-done = bf16[320,1024]{1,0:T(8,128)(2,1)} async-done(((bf16[1280,1024]{1,0:T(8,128)(2,1)}), bf16[320,1024]{1,0:T(8,128)(2,1)}) %reduce-scatter.19.cloned.1.call-update) | async-done | bytes 655376 | tf_op jit(solution)/shard_map/reduce_scatter | solution.py:140
  705.4 25.5 %all-gather.27.cloned.1.call-done = bf16[1280,1024]{1,0:T(8,128)(2,1)} async-done(((bf16[320,1024]{1,0:T(8,128)(2,1)}), bf16[1280,1024]{1,0:T(8,128)(2,1)}) %all-gather.27.cloned.1.call-update) | async-done | bytes 2621456 | tf_op jit(solution)/shard_map/all_gather | solution.py:202
  744.3 16.7 %multiply_reduce_fusion.1 = (f32[4,1280]{1,0:T(4,128)S(1)}, f32[4,1280,1280]{1,2,0:T(8,128)}) fusion(f32[4,1280,1280]{1,2,0:T(8,128)} %get-tuple-element.129, f32[4,1280]{1,0:T(4,128)S(1)} %log_add_fusion.1, bf16[1280,4,64]{0,2,1:T(8,128)(2,1)S(1)} %bitcast.336, bf16[1280,3,4,64]{0,3,2,1:T(8,128)(2,1)} %bitcast.346), kind=kOutput, calls=%fused_computation.8 | convolution fusion | flops 858516480 | bytes 53780480 | tf_op jit(solution)/shard_map/qhe,khe->hqk/dot_general | solution.py:61
  761.0 22.2 %multiply_convert_fusion.1 = bf16[4,1280,1280]{1,2,0:T(8,128)(2,1)} fusion(f32[4,1280,1280]{1,2,0:T(8,128)} %get-tuple-element.132, f32[4,1280,1280]{1,2,0:T(8,128)} %get-tuple-element.129, f32[4,1280]{1,0:T(4,128)S(1)} %get-tuple-element.131, f32[4,1280]{1,0:T(4,128)S(1)} %log_add_fusion.1), kind=kLoop, calls=%fused_computation.7 | loop fusion | flops 26214400 | bytes 65576960 | tf_op jit(solution)/shard_map/convert_element_type | solution.py:65
  807.4 34.5 %reduce-scatter.23.cloned.1.call-done = bf16[320,1024]{1,0:T(8,128)(2,1)} async-done(((bf16[1280,1024]{1,0:T(8,128)(2,1)}), bf16[320,1024]{1,0:T(8,128)(2,1)}) %reduce-scatter.23.cloned.1.call-update) | async-done | bytes 655376 | tf_op jit(solution)/shard_map/reduce_scatter | solution.py:222
  847.4 25.7 %all-gather.29.cloned.1.call-done = bf16[1280,1024]{1,0:T(8,128)(2,1)} async-done(((bf16[320,1024]{1,0:T(8,128)(2,1)}), bf16[1280,1024]{1,0:T(8,128)(2,1)}) %all-gather.29.cloned.1.call-update) | async-done | bytes 2621456 | tf_op jit(solution)/shard_map/all_gather | solution.py:183
  888.7 34.8 %reduce-scatter.25.cloned.1.call-done = bf16[320,1024]{1,0:T(8,128)(2,1)} async-done(((bf16[1280,1024]{1,0:T(8,128)(2,1)}), bf16[320,1024]{1,0:T(8,128)(2,1)}) %reduce-scatter.25.cloned.1.call-update) | async-done | bytes 655376 | tf_op jit(solution)/shard_map/reduce_scatter | solution.py:191
  929.5 25.2 %all-gather.31.cloned.1.call-done = bf16[1280,1024]{1,0:T(8,128)(2,1)} async-done(((bf16[320,1024]{1,0:T(8,128)(2,1)}), bf16[1280,1024]{1,0:T(8,128)(2,1)}) %all-gather.31.cloned.1.call-update) | async-done | bytes 2621456 | tf_op jit(solution)/shard_map/all_gather | solution.py:202
  957.4 11.7 fusion.35
  969.1 16.6 %multiply_reduce_fusion = (f32[4,1280]{1,0:T(4,128)S(1)}, f32[4,1280,1280]{1,2,0:T(8,128)}) fusion(f32[4,1280,1280]{1,2,0:T(8,128)} %get-tuple-element.126, f32[4,1280]{1,0:T(4,128)S(1)} %log_add_fusion, bf16[1280,4,64]{0,2,1:T(8,128)(2,1)S(1)} %bitcast.338, bf16[1280,3,4,64]{0,3,2,1:T(8,128)(2,1)S(1)} %bitcast.341), kind=kOutput, calls=%fused_computation.5 | convolution fusion | flops 858516480 | bytes 53780480 | tf_op jit(solution)/shard_map/qhe,khe->hqk/dot_general | solution.py:61
  985.7 22.1 %multiply_convert_fusion = bf16[4,1280,1280]{1,2,0:T(8,128)(2,1)} fusion(f32[4,1280,1280]{1,2,0:T(8,128)} %get-tuple-element.134, f32[4,1280,1280]{1,2,0:T(8,128)} %get-tuple-element.126, f32[4,1280]{1,0:T(4,128)S(1)} %get-tuple-element.133, f32[4,1280]{1,0:T(4,128)S(1)} %log_add_fusion), kind=kLoop, calls=%fused_computation.4 | loop fusion | flops 26214400 | bytes 65576960 | tf_op jit(solution)/shard_map/convert_element_type | solution.py:65
  1086.9 131.2 %reduce-scatter.35.cloned.1.call-done = f32[2,128,1024]{2,1,0:T(8,128)} async-done(((f32[2,1024,1024]{2,1,0:T(8,128)}), f32[2,128,1024]{2,1,0:T(8,128)}) %reduce-scatter.35.cloned.1.call-update) | async-done | bytes 1048592 | tf_op jit(solution)/shard_map/reduce_scatter | solution.py:237
  1218.2 152.1 %reduce-scatter.31.cloned.1.call-done = f32[2,128,1024]{2,1,0:T(8,128)} async-done(((f32[2,1024,1024]{2,1,0:T(8,128)}), f32[2,128,1024]{2,1,0:T(8,128)}) %reduce-scatter.31.cloned.1.call-update) | async-done | bytes 1048592 | tf_op jit(solution)/shard_map/reduce_scatter | solution.py:237
  1378.2 83.1 %reduce-scatter.33.cloned.1.call-done = f32[4,128,256]{1,2,0:T(8,128)} async-done(((f32[4,1024,256]{1,2,0:T(8,128)}), f32[4,128,256]{1,2,0:T(8,128)}) %reduce-scatter.33.cloned.1.call-update) | async-done | bytes 524304 | tf_op jit(solution)/shard_map/reduce_scatter | solution.py:236
  1461.4 92.2 %reduce-scatter.29.cloned.1.call-done = f32[4,128,256]{1,2,0:T(8,128)} async-done(((f32[4,1024,256]{1,2,0:T(8,128)}), f32[4,128,256]{1,2,0:T(8,128)}) %reduce-scatter.29.cloned.1.call-update) | async-done | bytes 524304 | tf_op jit(solution)/shard_map/reduce_scatter | solution.py:236
  1558.0 40.8 %all-reduce = (f32[1,6,2]{1,2,0:T(2,128)S(1)}, f32[1,6,2]{1,2,0:T(2,128)S(1)}, f32[1,4,1024]{2,1,0:T(4,128)S(1)}, f32[1,4,1024]{2,1,0:T(4,128)S(1)}) all-reduce(f32[1,6,2]{1,2,0:T(2,128)S(1)} %maximum_bitcast_fusion.2, f32[1,6,2]{1,2,0:T(2,128)S(1)} %maximum_bitcast_fusion.3, ...), channel_id=1, replica_groups=mesh['dp'=8,'mp'=4] {'dp','mp'}, use_global_device_ids=true, to_apply=%region_36.37 | all-reduce | flops 8216 | bytes 65728 | tf_op jit(solution)/shard_map/psum | solution.py:279
  (343 shorter events, 314.1 us)
Async XLA Ops:
  7.2 57.3 %all-gather.33.cloned.1.call-start = ((), (), s32[]{:S(2)}) async-start(), calls=%async_computation.32 | async-start | bytes 2359296 | tf_op jit(solution)/shard_map/all_gather | solution.py:108
  10.0 80.3 %all-gather.17.cloned.1.call-start = ((), (), s32[]{:S(2)}) async-start(), calls=%async_computation.12 | async-start | bytes 3276800 | tf_op jit(solution)/shard_map/all_gather | solution.py:118
  11.2 157.1 %copy-start.48 = (f32[1,1,1024]{2,1,0:T(1,128)}, f32[1,1,1024]{2,1,0:T(1,128)S(1)}, u32[]{:S(2)}) copy-start(f32[1,1,1024]{2,1,0:T(1,128)S(1)} %get-tuple-element.115) | copy-start | bytes 12292
  11.2 317.2 %copy-start.38 = (f32[1,1,1024]{2,1,0:T(1,128)}, f32[1,1,1024]{2,1,0:T(1,128)S(1)}, u32[]{:S(2)}) copy-start(f32[1,1,1024]{2,1,0:T(1,128)S(1)} %get-tuple-element.113) | copy-start | bytes 12292
  12.4 154.3 %reduce-scatter.13.cloned.1.call-start = ((), (), s32[]{:S(2)}) async-start(), calls=%async_computation.13 | async-start | bytes 3276800 | tf_op jit(solution)/shard_map/reduce_scatter | solution.py:127
  131.9 111.1 %all-gather.35.cloned.1.call-start = ((), (), s32[]{:S(2)}) async-start(), calls=%async_computation.33 | async-start | bytes 4718592 | tf_op jit(solution)/shard_map/all_gather | solution.py:109
  133.2 135.7 %all-gather.19.cloned.1.call-start = ((), (), s32[]{:S(2)}) async-start(), calls=%async_computation.14 | async-start | bytes 3276800 | tf_op jit(solution)/shard_map/all_gather | solution.py:137
  168.0 158.7 %copy-start.2 = (f32[320,1024]{1,0:T(8,128)}, f32[320,1024]{1,0:T(8,128)S(1)}, u32[]{:S(2)}) copy-start(f32[320,1024]{1,0:T(8,128)S(1)} %get-tuple-element.79) | copy-start | bytes 3932164
  168.0 118.1 %copy-start.51 = (f32[320]{0:T(512)}, f32[320]{0:T(512)S(1)}, u32[]{:S(2)}) copy-start(f32[320]{0:T(512)S(1)} %broadcast_multiply_fusion.2) | copy-start | bytes 3844
  168.3 117.8 %copy-start.64 = (f32[320]{0:T(512)}, f32[320]{0:T(512)S(1)}, u32[]{:S(2)}) copy-start(f32[320]{0:T(512)S(1)} %multiply_reduce_fusion.4) | copy-start | bytes 3844
  169.5 157.2 %reduce-scatter.15.cloned.1.call-start = ((), (), s32[]{:S(2)}) async-start(), calls=%async_computation.15 | async-start | bytes 3276800 | tf_op jit(solution)/shard_map/reduce_scatter | solution.py:140
  291.9 88.6 %all-gather.37.cloned.1.call-start = ((), (), s32[]{:S(2)}) async-start(), calls=%async_computation.34 | async-start | bytes 2359296 | tf_op jit(solution)/shard_map/all_gather | solution.py:108
  292.6 113.7 %all-gather.21.cloned.1.call-start = ((), (), s32[]{:S(2)}) async-start(), calls=%async_computation.16 | async-start | bytes 3276800 | tf_op jit(solution)/shard_map/all_gather | solution.py:118
  329.5 153.0 %reduce-scatter.17.cloned.1.call-start = ((), (), s32[]{:S(2)}) async-start(), calls=%async_computation.17 | async-start | bytes 3276800 | tf_op jit(solution)/shard_map/reduce_scatter | solution.py:127
  447.7 111.1 %all-gather.39.cloned.1.call-start = ((), (), s32[]{:S(2)}) async-start(), calls=%async_computation.35 | async-start | bytes 4718592 | tf_op jit(solution)/shard_map/all_gather | solution.py:109
  448.3 136.6 %all-gather.23.cloned.1.call-start = ((), (), s32[]{:S(2)}) async-start(), calls=%async_computation.18 | async-start | bytes 3276800 | tf_op jit(solution)/shard_map/all_gather | solution.py:137
  485.3 127.2 %all-gather.25.cloned.1.call-start = ((), (), s32[]{:S(2)}) async-start(), calls=%async_computation.20 | async-start | bytes 3276800 | tf_op jit(solution)/shard_map/all_gather | solution.py:183
  487.6 175.3 %reduce-scatter.21.cloned.1.call-start = ((), (), s32[]{:S(2)}) async-start(), calls=%async_computation.21 | async-start | bytes 3276800 | tf_op jit(solution)/shard_map/reduce_scatter | solution.py:191
  628.1 71.9 %reduce-scatter.19.cloned.1.call-start = ((), (), s32[]{:S(2)}) async-start(), calls=%async_computation.19 | async-start | bytes 3276800 | tf_op jit(solution)/shard_map/reduce_scatter | solution.py:140
  635.0 95.9 %all-gather.27.cloned.1.call-start = ((), (), s32[]{:S(2)}) async-start(), calls=%async_computation.22 | async-start | bytes 3276800 | tf_op jit(solution)/shard_map/all_gather | solution.py:202
  705.1 136.9 %reduce-scatter.23.cloned.1.call-start = ((), (), s32[]{:S(2)}) async-start(), calls=%async_computation.23 | async-start | bytes 3276800 | tf_op jit(solution)/shard_map/reduce_scatter | solution.py:222
  807.2 65.8 %all-gather.29.cloned.1.call-start = ((), (), s32[]{:S(2)}) async-start(), calls=%async_computation.24 | async-start | bytes 3276800 | tf_op jit(solution)/shard_map/all_gather | solution.py:183
  847.3 76.2 %reduce-scatter.25.cloned.1.call-start = ((), (), s32[]{:S(2)}) async-start(), calls=%async_computation.25 | async-start | bytes 3276800 | tf_op jit(solution)/shard_map/reduce_scatter | solution.py:191
  888.7 66.0 %all-gather.31.cloned.1.call-start = ((), (), s32[]{:S(2)}) async-start(), calls=%async_computation.26 | async-start | bytes 3276800 | tf_op jit(solution)/shard_map/all_gather | solution.py:202
  929.0 151.0 %reduce-scatter.27.cloned.1.call-start = ((), (), s32[]{:S(2)}) async-start(), calls=%async_computation.27 | async-start | bytes 3276800 | tf_op jit(solution)/shard_map/reduce_scatter | solution.py:222
  1030.6 187.5 %reduce-scatter.35.cloned.1.call-start = ((), (), s32[]{:S(2)}) async-start(), calls=%async_computation.31 | async-start | bytes 9437184 | tf_op jit(solution)/shard_map/reduce_scatter | solution.py:237
  1043.7 326.5 %reduce-scatter.31.cloned.1.call-start = ((), (), s32[]{:S(2)}) async-start(), calls=%async_computation.29 | async-start | bytes 9437184 | tf_op jit(solution)/shard_map/reduce_scatter | solution.py:237
  1056.9 404.5 %reduce-scatter.33.cloned.1.call-start = ((), (), s32[]{:S(2)}) async-start(), calls=%async_computation.30 | async-start | bytes 4718592 | tf_op jit(solution)/shard_map/reduce_scatter | solution.py:236
  1066.2 487.4 %reduce-scatter.29.cloned.1.call-start = ((), (), s32[]{:S(2)}) async-start(), calls=%async_computation.28 | async-start | bytes 4718592 | tf_op jit(solution)/shard_map/reduce_scatter | solution.py:236
  1083.4 286.8 %copy-start.5 = (f32[2,2,128,1024]{3,2,1,0:T(8,128)S(1)}, f32[2,2,128,1024]{3,2,1,0:T(8,128)}, u32[]{:S(2)}) copy-start(f32[2,2,128,1024]{3,2,1,0:T(8,128)} %param.19) | copy-start | bytes 6291460
  1375.9 177.6 %copy-start.7 = (f32[2,4,128,256]{2,3,1,0:T(8,128)S(1)}, f32[2,4,128,256]{2,3,1,0:T(8,128)}, u32[]{:S(2)}) copy-start(f32[2,4,128,256]{2,3,1,0:T(8,128)} %copy-done.6) | copy-start | bytes 3145732
  1378.2 220.5 %copy-start.71 = (f32[6]{0:T(128)S(1)}, f32[6]{0:T(128)}, u32[]{:S(2)}) copy-start(f32[6]{0:T(128)} %constant.139) | copy-start | bytes 76
  (75 other events, 1116.5 us)
Sparse Core Ops, SparseCore 0:
  10.6 53.7 all-gather.32
  66.6 23.7 all-gather.16
  132.0 34.6 reduce-scatter.12
  169.6 73.3 all-gather.34
  245.0 23.8 all-gather.18
  292.0 34.6 reduce-scatter.14
  329.3 51.0 all-gather.36
  382.6 23.7 all-gather.20
  447.8 34.6 reduce-scatter.16
  485.4 73.3 all-gather.38
  561.0 23.8 all-gather.22
  586.9 25.5 all-gather.24
  628.3 34.6 reduce-scatter.20
  665.3 34.6 reduce-scatter.18
  705.2 25.5 all-gather.26
  807.3 34.6 reduce-scatter.22
  847.4 25.5 all-gather.28
  888.8 34.6 reduce-scatter.24
  929.1 25.5 all-gather.30
  1030.7 34.6 reduce-scatter.26
  1069.1 149.0 reduce-scatter.34
  1222.2 147.9 reduce-scatter.30
  1373.9 87.4 reduce-scatter.32
  1465.3 88.2 reduce-scatter.28
where the time goes:
time: 1630 us; the launch traced here: 1620 us
  waiting for transfers between devices  1120 us (69%)
  matrix products  266 us (16%)
  other arithmetic  138 us (8%)
  blocking collectives  40.8 us (3%)
  local copies, waits for them, and re-layouts  31 us (2%)
    reduce_scatter x2, waiting for transfers between devices, shards(): lax.psum_scatter(dense_grad, 'dp', scatter_dimension=1, tiled=True)  283 us
    reduce_scatter x2, waiting for transfers between devices, shards(): lax.psum_scatter(mixer_grad, 'dp', scatter_dimension=1, tiled=True)  175 us
    all_gather x2, waiting for transfers between devices, shards(): lax.all_gather(dense_low[current], 'dp', axis=1, tiled=True)  134 us
    all_gather x2, waiting for transfers between devices, shards(): lax.all_gather(mixer_low[current], 'dp', axis=1, tiled=True)  102 us
    all_gather x4, waiting for transfers between devices, shards(): lax.all_gather(stream_grad.astype(jnp.bfloat16), 'mp', axis=0, tiled=True)  86.7 us
    reduce_scatter x2, waiting for transfers between devices, shards(): lax.psum_scatter(jnp.einsum('tf,df->td', active, dense_full[1], preferred...  68.9 us
    reduce_scatter x2, waiting for transfers between devices, shards(): lax.psum_scatter(jnp.einsum('th,dh->td', attended, mixer_full[3], preferr...  67.7 us
    reduce_scatter x2, waiting for transfers between devices, shards(): lax.psum_scatter(jnp.einsum('tf,df->td', grad_hidden, dense_full[0], pref...  62.7 us
  transfers between devices with their start and end apart: 24, of which 23 were waited for; matrix products, arithmetic and copies ran while one was open for 6% of the time, Pallas kernels for 0%

commit v1 on v0

--- a/solution.py
+++ b/solution.py
@@ -15,6 +15,17 @@
 WEIGHT_DECAY = 0.01
 LEARN_RATE = 0.5
 MASKED = -1000000000.0
+
+
+def gather_by_hops(value, name, dim):
+    devices = lax.axis_size(name)
+    route = [(i, (i + 1) % devices) for i in range(devices)]
+    blocks = [value]
+    for reach in range(1, devices):
+        blocks = [lax.ppermute(blocks[0], name, route), *blocks]
+    out = jnp.concatenate(blocks, axis=dim)
+    shift = (lax.axis_index(name) + 1) * blocks[-1].shape[dim]
+    return jnp.roll(out, shift, axis=dim)
 
 
 def layer_norm(stream, gain, shift):
@@ -134,7 +145,7 @@
         ).astype(jnp.float32)
         normed_two = layer_norm(middle, params[2], params[3]).astype(jnp.bfloat16)
         dense_wide = dense_full
-        gathered_two = lax.all_gather(normed_two, "mp", axis=0, tiled=True)
+        gathered_two = gather_by_hops(normed_two, "mp", 0)
         hidden = jnp.dot(gathered_two, dense_full[0], preferred_element_type=jnp.float32)
         active = gelu_exact(hidden).astype(jnp.bfloat16)
         after_dense = middle + lax.psum_scatter(

time: 1630 us -> 1580 us (0.969)
  waiting for transfers between devices: 1120 us -> 1040 us
  other arithmetic: 138 us -> 166 us
    all_gather x2, waiting for transfers between devices: 134 us -> 56.1 us  [shards(): lax.all_gather(dense_low[current], 'dp', axis=1, tiled=True)]
    ppermute x0 -> x6, waiting for transfers between devices: none -> 58.2 us  [gather_by_hops(): blocks = [lax.ppermute(blocks[0], name, route), *blocks]]
    all_gather x2 -> x0, waiting for transfers between devices: 52 us -> none  [shards(): gathered_two = lax.all_gather(normed_two, 'mp', axis=0, tiled=True)]
    concatenate x0 -> x2, other arithmetic: none -> 30 us  [gather_by_hops(): return jnp.roll(out, shift, axis=dim)]
  transfers between devices with their start and end apart: 24 -> 28, of which waited for: 23 -> 27; matrix products, arithmetic and copies ran while one was open for 6% -> 8% of each run, Pallas kernels for 0% -> 0%
where the time goes in v1:
time: 1580 us; the launch traced here: 1570 us
  waiting for transfers between devices  1040 us (66%)
  matrix products  265 us (17%)
  other arithmetic  166 us (11%)
  blocking collectives  40.8 us (3%)
  local copies, waits for them, and re-layouts  37 us (2%)
  between operations  16 us (1%)
    reduce_scatter x2, waiting for transfers between devices, shards(): lax.psum_scatter(dense_grad, 'dp', scatter_dimension=1, tiled=True)  281 us
    reduce_scatter x2, waiting for transfers between devices, shards(): lax.psum_scatter(mixer_grad, 'dp', scatter_dimension=1, tiled=True)  175 us
    all_gather x2, waiting for transfers between devices, shards(): lax.all_gather(mixer_low[current], 'dp', axis=1, tiled=True)  102 us
    all_gather x4, waiting for transfers between devices, shards(): lax.all_gather(stream_grad.astype(jnp.bfloat16), 'mp', axis=0, tiled=True)  84.8 us
    reduce_scatter x2, waiting for transfers between devices, shards(): lax.psum_scatter(jnp.einsum('th,dh->td', attended, mixer_full[3], preferr...  67.5 us
    reduce_scatter x2, waiting for transfers between devices, shards(): lax.psum_scatter(jnp.einsum('tf,df->td', active, dense_full[1], preferred...  67.4 us
    reduce_scatter x2, waiting for transfers between devices, shards(): lax.psum_scatter(jnp.einsum('tf,df->td', grad_hidden, dense_full[0], pref...  62.6 us
    ppermute x6, waiting for transfers between devices, gather_by_hops(): blocks = [lax.ppermute(blocks[0], name, route), *blocks]  58.2 us
  transfers between devices with their start and end apart: 28, of which 27 were waited for; matrix products, arithmetic and copies ran while one was open for 8% of the time, Pallas kernels for 0%

profile of v1, /device:TPU:0, one launch (start us, length us, event | category | flops | bytes accessed | tf_op | source)
XLA Modules:
  0.0 1570.4 jit_solution(14997162840254335896)
XLA Ops:
  13.5 51.0 %all-gather.27.cloned.1.call-done = bf16[1,4,1024,256]{2,3,1,0:T(8,128)(2,1)} async-done(((bf16[1,4,128,256]{2,3,1,0:T(8,128)(2,1)}), bf16[1,4,1024,256]{2,3,1,0:T(8,128)(2,1)}) %all-gather.27.cloned.1.call-update) | async-done | bytes 2097168 | tf_op jit(solution)/shard_map/all_gather | solution.py:119
  64.4 25.9 %all-gather.15.cloned.1.call-done = bf16[1280,1024]{1,0:T(8,128)(2,1)} async-done(((bf16[320,1024]{1,0:T(8,128)(2,1)}), bf16[1280,1024]{1,0:T(8,128)(2,1)}) %all-gather.15.cloned.1.call-update) | async-done | bytes 2621456 | tf_op jit(solution)/shard_map/all_gather | solution.py:129
  94.8 11.0 fusion.135
  116.5 11.0 fusion.57
  133.2 33.5 %reduce-scatter.13.cloned.1.call-done = bf16[320,1024]{1,0:T(8,128)(2,1)} async-done(((bf16[1280,1024]{1,0:T(8,128)(2,1)}), bf16[320,1024]{1,0:T(8,128)(2,1)}) %reduce-scatter.13.cloned.1.call-update) | async-done | bytes 655376 | tf_op jit(solution)/shard_map/reduce_scatter | solution.py:138
  200.0 16.8 %fusion.36 = bf16[1280,1024]{1,0:T(8,128)(2,1)} fusion(s32[]{:T(128)S(6)} %select_n.24, bf16[320,1024]{1,0:T(8,128)(2,1)} %collective-permute-done.2, bf16[320,1024]{1,0:T(8,128)(2,1)S(1)} %collective-permute-done.1, bf16[320,1024]{1,0:T(8,128)(2,1)S(1)} %collective-permute-done, bf16[320,1024]{1,0:T(8,128)(2,1)S(1)} %add_convert_fusion.4), kind=kLoop, calls=%fused_computation.103 | loop fusion | flops 20971520 | bytes 5242884 | tf_op jit(solution)/shard_map/jit(_roll_dynamic)/concatenate | solution.py:28
  216.8 26.1 %all-gather.29.cloned.1.call-done = bf16[1,2,1024,1024]{3,2,1,0:T(8,128)(2,1)} async-done(((bf16[1,2,128,1024]{3,2,1,0:T(8,128)(2,1)}), bf16[1,2,1024,1024]{3,2,1,0:T(8,128)(2,1)}) %all-gather.29.cloned.1.call-update) | async-done | bytes 4194320 | tf_op jit(solution)/shard_map/all_gather | solution.py:120
  243.0 17.3 %multiply_convert_fusion.3 = (bf16[1280,1024]{1,0:T(8,128)(2,1)S(1)}, f32[1280,1024]{1,0:T(8,128)}, f32[1280,1024]{1,0:T(8,128)}) fusion(bf16[1280,1024]{1,0:T(8,128)(2,1)} %fusion.36, bf16[1,2,1024,1024]{3,2,1,0:T(8,128)(2,1)} %all-gather.29.cloned.1.call-done), kind=kOutput, calls=%fused_computation.63 | convolution fusion | flops 2769551360 | bytes 17825792 | tf_op jit(solution)/shard_map/dot_general | solution.py:149
  266.8 32.5 %reduce-scatter.15.cloned.1.call-done = bf16[320,1024]{1,0:T(8,128)(2,1)} async-done(((bf16[1280,1024]{1,0:T(8,128)(2,1)}), bf16[320,1024]{1,0:T(8,128)(2,1)}) %reduce-scatter.15.cloned.1.call-update) | async-done | bytes 655376 | tf_op jit(solution)/shard_map/reduce_scatter | solution.py:151
  302.1 50.7 %all-gather.31.cloned.1.call-done = bf16[1,4,1024,256]{2,3,1,0:T(8,128)(2,1)} async-done(((bf16[1,4,128,256]{2,3,1,0:T(8,128)(2,1)}), bf16[1,4,1024,256]{2,3,1,0:T(8,128)(2,1)}) %all-gather.31.cloned.1.call-update) | async-done | bytes 2097168 | tf_op jit(solution)/shard_map/all_gather | solution.py:119
  352.9 25.9 %all-gather.17.cloned.1.call-done = bf16[1280,1024]{1,0:T(8,128)(2,1)} async-done(((bf16[320,1024]{1,0:T(8,128)(2,1)}), bf16[1280,1024]{1,0:T(8,128)(2,1)}) %all-gather.17.cloned.1.call-update) | async-done | bytes 2621456 | tf_op jit(solution)/shard_map/all_gather | solution.py:129
  420.9 34.0 %reduce-scatter.17.cloned.1.call-done = bf16[320,1024]{1,0:T(8,128)(2,1)} async-done(((bf16[1280,1024]{1,0:T(8,128)(2,1)}), bf16[320,1024]{1,0:T(8,128)(2,1)}) %reduce-scatter.17.cloned.1.call-update) | async-done | bytes 655376 | tf_op jit(solution)/shard_map/reduce_scatter | solution.py:138
  488.2 13.2 fusion.29
  501.4 30.0 %all-gather.33.cloned.1.call-done = bf16[1,2,1024,1024]{3,2,1,0:T(8,128)(2,1)} async-done(((bf16[1,2,128,1024]{3,2,1,0:T(8,128)(2,1)}), bf16[1,2,1024,1024]{3,2,1,0:T(8,128)(2,1)}) %all-gather.33.cloned.1.call-update) | async-done | bytes 4194320 | tf_op jit(solution)/shard_map/all_gather | solution.py:120
  531.3 17.7 %multiply_convert_fusion.2 = (bf16[1280,1024]{1,0:T(8,128)(2,1)}, f32[1280,1024]{1,0:T(8,128)}, f32[1280,1024]{1,0:T(8,128)}) fusion(bf16[1280,1024]{1,0:T(8,128)(2,1)} %fusion.29, bf16[1,2,1024,1024]{3,2,1,0:T(8,128)(2,1)} %all-gather.33.cloned.1.call-done), kind=kOutput, calls=%fused_computation.50 | convolution fusion | flops 2769551360 | bytes 17825792 | tf_op jit(solution)/shard_map/dot_general | solution.py:149
  579.9 27.9 %reduce-scatter.21.cloned.1.call-done = bf16[320,1024]{1,0:T(8,128)(2,1)} async-done(((bf16[1280,1024]{1,0:T(8,128)(2,1)}), bf16[320,1024]{1,0:T(8,128)(2,1)}) %reduce-scatter.21.cloned.1.call-update) | async-done | bytes 655376 | tf_op jit(solution)/shard_map/reduce_scatter | solution.py:202
  609.9 34.9 %reduce-scatter.19.cloned.1.call-done = bf16[320,1024]{1,0:T(8,128)(2,1)} async-done(((bf16[1280,1024]{1,0:T(8,128)(2,1)}), bf16[320,1024]{1,0:T(8,128)(2,1)}) %reduce-scatter.19.cloned.1.call-update) | async-done | bytes 655376 | tf_op jit(solution)/shard_map/reduce_scatter | solution.py:151
  650.0 25.6 %all-gather.21.cloned.1.call-done = bf16[1280,1024]{1,0:T(8,128)(2,1)} async-done(((bf16[320,1024]{1,0:T(8,128)(2,1)}), bf16[1280,1024]{1,0:T(8,128)(2,1)}) %all-gather.21.cloned.1.call-update) | async-done | bytes 2621456 | tf_op jit(solution)/shard_map/all_gather | solution.py:213
  689.2 16.7 %multiply_reduce_fusion.1 = (f32[4,1280]{1,0:T(4,128)S(1)}, f32[4,1280,1280]{1,2,0:T(8,128)}) fusion(f32[4,1280,1280]{1,2,0:T(8,128)} %get-tuple-element.130, f32[4,1280]{1,0:T(4,128)S(1)} %log_add_fusion.1, bf16[1280,4,64]{0,2,1:T(8,128)(2,1)S(1)} %bitcast.336, bf16[1280,3,4,64]{0,3,2,1:T(8,128)(2,1)} %bitcast.346), kind=kOutput, calls=%fused_computation.8 | convolution fusion | flops 858516480 | bytes 53780480 | tf_op jit(solution)/shard_map/qhe,khe->hqk/dot_general | solution.py:72
  705.9 22.2 %multiply_convert_fusion.1 = bf16[4,1280,1280]{1,2,0:T(8,128)(2,1)} fusion(f32[4,1280,1280]{1,2,0:T(8,128)} %get-tuple-element.133, f32[4,1280,1280]{1,2,0:T(8,128)} %get-tuple-element.130, f32[4,1280]{1,0:T(4,128)S(1)} %get-tuple-element.132, f32[4,1280]{1,0:T(4,128)S(1)} %log_add_fusion.1), kind=kLoop, calls=%fused_computation.7 | loop fusion | flops 26214400 | bytes 65576960 | tf_op jit(solution)/shard_map/convert_element_type | solution.py:76
  752.3 34.5 %reduce-scatter.23.cloned.1.call-done = bf16[320,1024]{1,0:T(8,128)(2,1)} async-done(((bf16[1280,1024]{1,0:T(8,128)(2,1)}), bf16[320,1024]{1,0:T(8,128)(2,1)}) %reduce-scatter.23.cloned.1.call-update) | async-done | bytes 655376 | tf_op jit(solution)/shard_map/reduce_scatter | solution.py:233
  792.2 25.7 %all-gather.23.cloned.1.call-done = bf16[1280,1024]{1,0:T(8,128)(2,1)} async-done(((bf16[320,1024]{1,0:T(8,128)(2,1)}), bf16[1280,1024]{1,0:T(8,128)(2,1)}) %all-gather.23.cloned.1.call-update) | async-done | bytes 2621456 | tf_op jit(solution)/shard_map/all_gather | solution.py:194
  833.6 34.8 %reduce-scatter.25.cloned.1.call-done = bf16[320,1024]{1,0:T(8,128)(2,1)} async-done(((bf16[1280,1024]{1,0:T(8,128)(2,1)}), bf16[320,1024]{1,0:T(8,128)(2,1)}) %reduce-scatter.25.cloned.1.call-update) | async-done | bytes 655376 | tf_op jit(solution)/shard_map/reduce_scatter | solution.py:202
  874.3 25.2 %all-gather.25.cloned.1.call-done = bf16[1280,1024]{1,0:T(8,128)(2,1)} async-done(((bf16[320,1024]{1,0:T(8,128)(2,1)}), bf16[1280,1024]{1,0:T(8,128)(2,1)}) %all-gather.25.cloned.1.call-update) | async-done | bytes 2621456 | tf_op jit(solution)/shard_map/all_gather | solution.py:213
  902.3 11.7 fusion.49
  914.0 16.6 %multiply_reduce_fusion = (f32[4,1280]{1,0:T(4,128)S(1)}, f32[4,1280,1280]{1,2,0:T(8,128)}) fusion(f32[4,1280,1280]{1,2,0:T(8,128)} %get-tuple-element.127, f32[4,1280]{1,0:T(4,128)S(1)} %log_add_fusion, bf16[1280,4,64]{0,2,1:T(8,128)(2,1)S(1)} %bitcast.338, bf16[1280,3,4,64]{0,3,2,1:T(8,128)(2,1)S(1)} %bitcast.341), kind=kOutput, calls=%fused_computation.5 | convolution fusion | flops 858516480 | bytes 53780480 | tf_op jit(solution)/shard_map/qhe,khe->hqk/dot_general | solution.py:72
  930.5 22.0 %multiply_convert_fusion = bf16[4,1280,1280]{1,2,0:T(8,128)(2,1)} fusion(f32[4,1280,1280]{1,2,0:T(8,128)} %get-tuple-element.135, f32[4,1280,1280]{1,2,0:T(8,128)} %get-tuple-element.127, f32[4,1280]{1,0:T(4,128)S(1)} %get-tuple-element.134, f32[4,1280]{1,0:T(4,128)S(1)} %log_add_fusion), kind=kLoop, calls=%fused_computation.4 | loop fusion | flops 26214400 | bytes 65576960 | tf_op jit(solution)/shard_map/convert_element_type | solution.py:76
  1034.5 129.0 %reduce-scatter.35.cloned.1.call-done = f32[2,128,1024]{2,1,0:T(8,128)} async-done(((f32[2,1024,1024]{2,1,0:T(8,128)}), f32[2,128,1024]{2,1,0:T(8,128)}) %reduce-scatter.35.cloned.1.call-update) | async-done | bytes 1048592 | tf_op jit(solution)/shard_map/reduce_scatter | solution.py:248
  1163.5 151.9 %reduce-scatter.31.cloned.1.call-done = f32[2,128,1024]{2,1,0:T(8,128)} async-done(((f32[2,1024,1024]{2,1,0:T(8,128)}), f32[2,128,1024]{2,1,0:T(8,128)}) %reduce-scatter.31.cloned.1.call-update) | async-done | bytes 1048592 | tf_op jit(solution)/shard_map/reduce_scatter | solution.py:248
  1323.5 83.2 %reduce-scatter.33.cloned.1.call-done = f32[4,128,256]{1,2,0:T(8,128)} async-done(((f32[4,1024,256]{1,2,0:T(8,128)}), f32[4,128,256]{1,2,0:T(8,128)}) %reduce-scatter.33.cloned.1.call-update) | async-done | bytes 524304 | tf_op jit(solution)/shard_map/reduce_scatter | solution.py:247
  1406.6 92.3 %reduce-scatter.29.cloned.1.call-done = f32[4,128,256]{1,2,0:T(8,128)} async-done(((f32[4,1024,256]{1,2,0:T(8,128)}), f32[4,128,256]{1,2,0:T(8,128)}) %reduce-scatter.29.cloned.1.call-update) | async-done | bytes 524304 | tf_op jit(solution)/shard_map/reduce_scatter | solution.py:247
  1503.4 40.8 %all-reduce = (f32[1,6,2]{1,2,0:T(2,128)S(1)}, f32[1,6,2]{1,2,0:T(2,128)S(1)}, f32[1,4,1024]{2,1,0:T(4,128)S(1)}, f32[1,4,1024]{2,1,0:T(4,128)S(1)}) all-reduce(f32[1,6,2]{1,2,0:T(2,128)S(1)} %maximum_bitcast_fusion.2, f32[1,6,2]{1,2,0:T(2,128)S(1)} %maximum_bitcast_fusion.3, ...), channel_id=1, replica_groups=mesh['dp'=8,'mp'=4] {'dp','mp'}, use_global_device_ids=true, to_apply=%region_36.38 | all-reduce | flops 8216 | bytes 65728 | tf_op jit(solution)/shard_map/psum | solution.py:290
  (363 shorter events, 362.7 us)
Async XLA Ops:
  7.2 57.3 %all-gather.27.cloned.1.call-start = ((), (), s32[]{:S(2)}) async-start(), calls=%async_computation.30 | async-start | bytes 2359296 | tf_op jit(solution)/shard_map/all_gather | solution.py:119
  10.0 80.3 %all-gather.15.cloned.1.call-start = ((), (), s32[]{:S(2)}) async-start(), calls=%async_computation.12 | async-start | bytes 3276800 | tf_op jit(solution)/shard_map/all_gather | solution.py:129
  11.2 289.7 %copy-start.44 = (f32[1,1,1024]{2,1,0:T(1,128)}, f32[1,1,1024]{2,1,0:T(1,128)S(1)}, u32[]{:S(2)}) copy-start(f32[1,1,1024]{2,1,0:T(1,128)S(1)} %get-tuple-element.114) | copy-start | bytes 12292
  12.4 154.3 %reduce-scatter.13.cloned.1.call-start = ((), (), s32[]{:S(2)}) async-start(), calls=%async_computation.13 | async-start | bytes 3276800 | tf_op jit(solution)/shard_map/reduce_scatter | solution.py:138
  131.9 111.1 %all-gather.29.cloned.1.call-start = ((), (), s32[]{:S(2)}) async-start(), calls=%async_computation.31 | async-start | bytes 4718592 | tf_op jit(solution)/shard_map/all_gather | solution.py:120
  133.2 166.1 %reduce-scatter.15.cloned.1.call-start = ((), (), s32[]{:S(2)}) async-start(), calls=%async_computation.14 | async-start | bytes 3276800 | tf_op jit(solution)/shard_map/reduce_scatter | solution.py:151
  169.4 10.1 collective-permute-start
  179.4 10.0 collective-permute-start.1
  189.4 10.6 collective-permute-start.2
  266.2 86.7 %all-gather.31.cloned.1.call-start = ((), (), s32[]{:S(2)}) async-start(), calls=%async_computation.32 | async-start | bytes 2359296 | tf_op jit(solution)/shard_map/all_gather | solution.py:119
  266.7 112.0 %all-gather.17.cloned.1.call-start = ((), (), s32[]{:S(2)}) async-start(), calls=%async_computation.15 | async-start | bytes 3276800 | tf_op jit(solution)/shard_map/all_gather | solution.py:129
  302.1 152.8 %reduce-scatter.17.cloned.1.call-start = ((), (), s32[]{:S(2)}) async-start(), calls=%async_computation.16 | async-start | bytes 3276800 | tf_op jit(solution)/shard_map/reduce_scatter | solution.py:138
  420.1 111.2 %all-gather.33.cloned.1.call-start = ((), (), s32[]{:S(2)}) async-start(), calls=%async_computation.33 | async-start | bytes 4718592 | tf_op jit(solution)/shard_map/all_gather | solution.py:120
  420.8 136.4 %all-gather.19.cloned.1.call-start = ((), (), s32[]{:S(2)}) async-start(), calls=%async_computation.18 | async-start | bytes 3276800 | tf_op jit(solution)/shard_map/all_gather | solution.py:194
  456.8 10.1 collective-permute-start.3
  467.7 10.1 collective-permute-start.4
  477.9 10.3 collective-permute-start.5
  480.2 127.6 %reduce-scatter.21.cloned.1.call-start = ((), (), s32[]{:S(2)}) async-start(), calls=%async_computation.19 | async-start | bytes 3276800 | tf_op jit(solution)/shard_map/reduce_scatter | solution.py:202
  572.9 71.9 %reduce-scatter.19.cloned.1.call-start = ((), (), s32[]{:S(2)}) async-start(), calls=%async_computation.17 | async-start | bytes 3276800 | tf_op jit(solution)/shard_map/reduce_scatter | solution.py:151
  579.8 95.8 %all-gather.21.cloned.1.call-start = ((), (), s32[]{:S(2)}) async-start(), calls=%async_computation.20 | async-start | bytes 3276800 | tf_op jit(solution)/shard_map/all_gather | solution.py:213
  649.9 137.0 %reduce-scatter.23.cloned.1.call-start = ((), (), s32[]{:S(2)}) async-start(), calls=%async_computation.21 | async-start | bytes 3276800 | tf_op jit(solution)/shard_map/reduce_scatter | solution.py:233
  752.0 65.9 %all-gather.23.cloned.1.call-start = ((), (), s32[]{:S(2)}) async-start(), calls=%async_computation.22 | async-start | bytes 3276800 | tf_op jit(solution)/shard_map/all_gather | solution.py:194
  792.2 76.2 %reduce-scatter.25.cloned.1.call-start = ((), (), s32[]{:S(2)}) async-start(), calls=%async_computation.23 | async-start | bytes 3276800 | tf_op jit(solution)/shard_map/reduce_scatter | solution.py:202
  833.6 66.0 %all-gather.25.cloned.1.call-start = ((), (), s32[]{:S(2)}) async-start(), calls=%async_computation.24 | async-start | bytes 3276800 | tf_op jit(solution)/shard_map/all_gather | solution.py:213
  873.8 153.8 %reduce-scatter.27.cloned.1.call-start = ((), (), s32[]{:S(2)}) async-start(), calls=%async_computation.25 | async-start | bytes 3276800 | tf_op jit(solution)/shard_map/reduce_scatter | solution.py:233
  976.0 187.5 %reduce-scatter.35.cloned.1.call-start = ((), (), s32[]{:S(2)}) async-start(), calls=%async_computation.29 | async-start | bytes 9437184 | tf_op jit(solution)/shard_map/reduce_scatter | solution.py:248
  989.9 325.6 %reduce-scatter.31.cloned.1.call-start = ((), (), s32[]{:S(2)}) async-start(), calls=%async_computation.27 | async-start | bytes 9437184 | tf_op jit(solution)/shard_map/reduce_scatter | solution.py:248
  1003.7 403.0 %reduce-scatter.33.cloned.1.call-start = ((), (), s32[]{:S(2)}) async-start(), calls=%async_computation.28 | async-start | bytes 4718592 | tf_op jit(solution)/shard_map/reduce_scatter | solution.py:247
  1013.7 485.3 %reduce-scatter.29.cloned.1.call-start = ((), (), s32[]{:S(2)}) async-start(), calls=%async_computation.26 | async-start | bytes 4718592 | tf_op jit(solution)/shard_map/reduce_scatter | solution.py:247
  1031.0 284.5 %copy-start.5 = (f32[2,2,128,1024]{3,2,1,0:T(8,128)S(1)}, f32[2,2,128,1024]{3,2,1,0:T(8,128)}, u32[]{:S(2)}) copy-start(f32[2,2,128,1024]{3,2,1,0:T(8,128)} %param.21) | copy-start | bytes 6291460
  1321.1 177.8 %copy-start.7 = (f32[2,4,128,256]{2,3,1,0:T(8,128)S(1)}, f32[2,4,128,256]{2,3,1,0:T(8,128)}, u32[]{:S(2)}) copy-start(f32[2,4,128,256]{2,3,1,0:T(8,128)} %copy-done.6) | copy-start | bytes 3145732
  1323.5 220.7 %copy-start.77 = (f32[6]{0:T(128)S(1)}, f32[6]{0:T(128)}, u32[]{:S(2)}) copy-start(f32[6]{0:T(128)} %constant.161) | copy-start | bytes 76
  (85 other events, 1293.1 us)
Sparse Core Ops, SparseCore 0:
  10.6 53.7 all-gather.26
  66.6 23.7 all-gather.14
  132.0 34.6 reduce-scatter.12
  169.6 73.3 all-gather.28
  266.3 32.9 reduce-scatter.14
  301.7 51.0 all-gather.30
  355.0 23.7 all-gather.16
  420.2 34.6 reduce-scatter.16
  457.9 73.3 all-gather.32
  533.4 23.8 all-gather.18
  573.0 34.6 reduce-scatter.20
  610.1 34.6 reduce-scatter.18
  650.0 25.5 all-gather.20
  752.1 34.6 reduce-scatter.22
  792.3 25.5 all-gather.22
  833.7 34.6 reduce-scatter.24
  873.9 25.5 all-gather.24
  976.2 34.6 reduce-scatter.26
  1014.5 149.0 reduce-scatter.34
  1167.5 147.9 reduce-scatter.30
  1319.1 87.4 reduce-scatter.32
  1410.7 88.1 reduce-scatter.28
